TPU v7x, 32 devices: a whole 2x2x4 slice. The times are simulated.
32 devices in a mesh: groups: 2 (over x), seq: 16 (over z, y, core).
Axes of the slice: x: 2, y: 2, z: 4, core: 2. Of those that a mesh axis runs over, the one named last changes fastest.
Arguments:
- latent: bfloat16 [32, 32768], P(('groups', 'seq')), parts along dimension 0, may hold values from -6 to 6
- text_embed: bfloat16 [4, 128, 3072], P('groups'), parts along dimension 0, may hold values from -6 to 6
- text_mask: int32 [4, 128], P('groups'), parts along dimension 0, may hold values from 0 to 1, as said below
- modulation: float32 [4, 5, 3072], P('groups'), parts along dimension 0, may hold values from -3 to 10
- w_in: bfloat16 [64, 3072], replicated, may hold values from -0.75 to 0.75
- w_qkv: bfloat16 [3072, 4608], P(None, 'seq'), may hold values from -0.109375 to 0.109375
- w_attn_out: bfloat16 [1536, 3072], P(None, 'seq'), may hold values from -0.15625 to 0.15625
- w_final: bfloat16 [3072, 64], replicated, may hold values from -0.109375 to 0.109375
Outputs:
- guided: float32 [32, 32768], P(('groups', 'seq')), parts along dimension 0
There are 2 independent parts, one for each index of `groups`. A program takes and returns all parts, laid end to end along the dimension named above; an argument that names none is the same for every part. Nothing has to cross between parts.
Inputs may be any that keep to these rules, and one draw needn't show every extreme that they name: `text_mask`: each row is 1 on a leading run of 1 to 127 positions and 0 after it.
All inputs are finite; a program needn't handle non-finite values.
Results may differ from a plain program's by a relative error of at most 0.007.
The roundings to bfloat16 on the way count: a program that leaves them out, or rounds other values in their place, can miss the bound.
Values may be sent and summed in bfloat16 or wider, within the bound.
A program may use at most 128 MiB of HBM per device.

v0:
```python
import jax
import jax.numpy as jnp
from jax import lax
from jax.sharding import PartitionSpec as P

HDIM = 128
SHEADS = 6
THEADS = 6
CHAN = 64
HEADS = 12
EPS = 1e-06
GUIDE = 5.0


def normalize(values):
    center = values - jnp.mean(values, axis=-1, keepdims=True)
    spread = jnp.mean(center * center, axis=-1, keepdims=True)
    return center * lax.rsqrt(spread + EPS)


def attend(query, keys, values, live):
    scores = jnp.einsum("qhe,khe->hqk", query, keys, preferred_element_type=jnp.float32) * HDIM ** (
        -0.5
    )
    scores = jnp.where(live[None, None, :], scores, -1e30)
    top = jnp.max(scores, axis=-1, keepdims=True)
    weights = jnp.exp(scores - top)
    total = jnp.sum(weights, axis=-1, keepdims=True)
    probs = weights.astype(jnp.bfloat16)
    mixed = jnp.einsum("hqk,khe->qhe", probs, values, preferred_element_type=jnp.float32)
    return (mixed / jnp.transpose(total, (1, 0, 2))).astype(jnp.bfloat16)


def temporal_mix(block):
    frames, span, heads = (block.shape[0], block.shape[1], block.shape[3])
    grid = block.reshape(2, frames // 2, span, 3, heads, HDIM)
    scores = jnp.einsum(
        "afpne,agpne->apnfg", grid[:, :, :, 0], grid[:, :, :, 1], preferred_element_type=jnp.float32
    ) * HDIM ** (-0.5)
    top = jnp.max(scores, axis=-1, keepdims=True)
    weights = jnp.exp(scores - top)
    total = jnp.sum(weights, axis=-1)
    probs = weights.astype(jnp.bfloat16)
    mixed = jnp.einsum(
        "apnfg,agpne->afpne", probs, grid[:, :, :, 2], preferred_element_type=jnp.float32
    )
    mixed = mixed / jnp.moveaxis(total, 3, 1)[..., None]
    return mixed.astype(jnp.bfloat16).reshape(frames, span, heads, HDIM)


def temporal_local(pieces):
    qkv_piece, spatial_piece, latent_piece = pieces
    frames_here, width = (qkv_piece.shape[0], qkv_piece.shape[2])
    mixed = temporal_mix(qkv_piece.reshape(frames_here, width, 3, THEADS, HDIM))
    return (mixed.reshape(frames_here, 1, width, THEADS * HDIM), spatial_piece, latent_piece)


def per_device(latent, text_embed, text_mask, modulation, w_in, w_qkv, w_attn_out, w_final):
    count = lax.axis_size("seq")
    index = lax.axis_index("seq")
    half = index // (count // 2)
    positions = latent.shape[1] // CHAN
    start = jnp.dot(latent.reshape(positions, CHAN), w_in, preferred_element_type=jnp.float32)
    mods = lax.dynamic_index_in_dim(modulation, half, 0, keepdims=False)
    hidden = (normalize(start) * (1.0 + mods[1]) + mods[0]).astype(jnp.bfloat16)
    words = lax.dynamic_index_in_dim(text_embed, half, 0, keepdims=False)
    valid = lax.dynamic_index_in_dim(text_mask, half, 0, keepdims=False) > 0
    rows = jnp.concatenate([hidden, words], axis=0)
    projected = jnp.dot(
        rows, lax.all_gather(w_qkv, "seq", axis=1, tiled=True), preferred_element_type=jnp.float32
    ).astype(jnp.bfloat16)
    projected = projected.reshape(rows.shape[0], 3, HEADS, HDIM)
    live = jnp.concatenate([jnp.ones((positions,), bool), valid])
    spatial_out = attend(
        projected[:positions, 0, :SHEADS], projected[:, 1, :SHEADS], projected[:, 2, :SHEADS], live
    )
    span = positions // count
    temporal_rows = projected[:positions, :, SHEADS:].reshape(1, count, span, 3 * THEADS * HDIM)
    spatial_rows = spatial_out.reshape(1, count, span, SHEADS * HDIM)
    latent_rows = latent.reshape(1, count, span, CHAN)
    temporal_pos, spatial_pos, latent_pos = temporal_local(
        (
            lax.all_to_all(temporal_rows, "seq", split_axis=1, concat_axis=0, tiled=True),
            lax.all_to_all(spatial_rows, "seq", split_axis=1, concat_axis=0, tiled=True),
            lax.all_to_all(latent_rows, "seq", split_axis=1, concat_axis=0, tiled=True),
        )
    )
    joined = jnp.concatenate(
        [
            spatial_pos.reshape(positions, SHEADS * HDIM),
            temporal_pos.reshape(positions, THEADS * HDIM),
        ],
        axis=1,
    )
    mixed_out = jnp.dot(
        joined,
        lax.all_gather(w_attn_out, "seq", axis=1, tiled=True),
        preferred_element_type=jnp.float32,
    )
    cond_side = (jnp.arange(count) < count // 2)[:, None, None]
    frame_mods = jnp.where(cond_side, modulation[0][None], modulation[1][None])
    start_here = jnp.dot(
        latent_pos.reshape(positions, CHAN), w_in, preferred_element_type=jnp.float32
    )
    block = start_here.reshape(count, span, -1) + frame_mods[:, 2][:, None, :] * mixed_out.reshape(
        count, span, -1
    )
    final = (
        normalize(block) * (1.0 + frame_mods[:, 4][:, None, :]) + frame_mods[:, 3][:, None, :]
    ).astype(jnp.bfloat16)
    pred = jnp.dot(
        final.reshape(positions, -1), w_final, preferred_element_type=jnp.float32
    ).astype(jnp.bfloat16)
    pred = lax.optimization_barrier(pred).astype(jnp.float32).reshape(count, span, CHAN)
    cond_pred = pred[: count // 2]
    uncond_pred = pred[count // 2 :]
    guided_here = uncond_pred + GUIDE * (cond_pred - uncond_pred)
    both_halves = jnp.concatenate([guided_here, guided_here], axis=0)
    result = lax.all_to_all(
        both_halves.astype(jnp.bfloat16), "seq", split_axis=0, concat_axis=1, tiled=True
    ).astype(both_halves.dtype)
    return result.reshape(1, positions * CHAN)


def solution(mesh):
    in_specs = (
        P(("groups", "seq"), None),
        P("groups", None, None),
        P("groups", None),
        P("groups", None, None),
        P(),
        P(None, "seq"),
        P(None, "seq"),
        P(),
    )
    out_specs = P(("groups", "seq"), None)
    return jax.shard_map(
        per_device, mesh=mesh, in_specs=in_specs, out_specs=out_specs, check_vma=False
    )
```

profile of v0, /device:TPU:0, one launch (start us, length us, event | category | flops | bytes accessed | tf_op | source)
XLA Modules:
  0.0 340.8 jit_solution(5030938691249247104)
XLA Ops:
  8.0 1.3 reduce
  9.4 0.8 reshape.119
  10.2 7.4 %all-to-all-start = ((bf16[16,2,1024]{2,1,0:T(2,128)(2,1)}), bf16[16,2,1024]{2,1,0:T(2,128)(2,1)S(1)}, u32[]{:S(2)}, u32[]{:S(2)}) async-start(bf16[16,2,1024]{2,1,0:T(2,128)(2,1)} %reshape.119), calls=%async_computation | async-start | bytes 131072 | tf_op jit(solution)/shard_map/all_to_all | solution.py:85
  17.7 2.2 fusion.35
  19.9 0.8 multiply_reduce_fusion.1
  20.8 3.3 add_convert_fusion.1
  24.1 132.0 %all-gather.3.cloned.1.call-done = bf16[3072,4608]{0,1:T(8,128)(2,1)} async-done(((bf16[3072,288]{0,1:T(8,128)(2,1)}), bf16[3072,4608]{0,1:T(8,128)(2,1)}) %all-gather.3.cloned.1.call-update) | async-done | bytes 28311568 | tf_op jit(solution)/shard_map/all_gather | solution.py:70
  156.1 24.7 %convolution_convert_fusion = bf16[640,4608]{1,0:T(8,128)(2,1)} fusion(bf16[3072,4608]{0,1:T(8,128)(2,1)} %all-gather.3.cloned.1.call-done, bf16[128,3072]{1,0:T(8,128)(2,1)S(1)} %dynamic-slice_bitcast_fusion, bf16[512,3072]{1,0:T(8,128)(2,1)} %add_convert_fusion.1), kind=kOutput, calls=%fused_computation | convolution fusion | flops 18130206720 | bytes 38141952 | tf_op jit(solution)/shard_map/dot_general | solution.py:69
  180.8 8.9 %copy.30 = bf16[640,4608]{0,1:T(8,128)(2,1)} copy(bf16[640,4608]{1,0:T(8,128)(2,1)} %convolution_convert_fusion) | data formatting | bytes 11796480 | tf_op jit(solution)/shard_map/convert_element_type | solution.py:71
  189.8 3.3 slice.78
  193.1 4.7 %copy.35 = bf16[512,3,6,128]{3,2,1,0:T(8,128)(2,1)} copy(bf16[512,3,6,128]{0,3,2,1:T(8,128)(2,1)} %slice.78) | data formatting | bytes 4718592 | tf_op jit(solution)/shard_map/slice | solution.py:78
  197.8 6.0 %reshape.112 = bf16[1,16,32,2304]{3,2,1,0:T(8,128)(2,1)} reshape(bf16[512,3,6,128]{3,2,1,0:T(8,128)(2,1)} %copy.35) | data formatting | bytes 4718592 | tf_op jit(solution)/shard_map/reshape | solution.py:78
  203.8 4.9 %all-to-all-start.2 = ((bf16[1,16,32,2304]{3,2,0,1:T(8,128)(2,1)}), bf16[1,16,32,2304]{3,2,0,1:T(8,128)(2,1)}, u32[]{:S(2)}, u32[]{:S(2)}) async-start(bf16[1,16,32,2304]{3,2,0,1:T(8,128)(2,1)} %bitcast.101), calls=%async_computation.2 | async-start | bytes 4718592 | tf_op jit(solution)/shard_map/all_to_all | solution.py:83
  209.0 3.0 fusion
  212.1 2.0 fusion.1
  214.1 3.5 %fusion.17 = bf16[512,6,128]{0,2,1:T(8,128)(2,1)S(1)} fusion(f32[6,512,640]{2,1,0:T(8,128)S(1)} %get-tuple-element.22, f32[6,512]{1,0:T(8,128)S(1)} %get-tuple-element.21, pred[640]{0:T(1024)(128)(4,1)S(1)} %concatenate.14, bf16[640,3,12,128]{0,3,2,1:T(8,128)(2,1)} %bitcast.99, f32[512,6]{0,1:T(8,128)S(1)} %bitcast.112), kind=kOutput, calls=%fused_computation.26 | convolution fusion | flops 511967232 | bytes 9659008 | tf_op jit(solution)/shard_map/hqk,khe->qhe/dot_general | solution.py:30
  218.4 1.8 reshape.110
  220.2 56.8 %all-to-all-done.2 = bf16[1,16,32,2304]{3,2,0,1:T(8,128)(2,1)} async-done(((bf16[1,16,32,2304]{3,2,0,1:T(8,128)(2,1)}), bf16[1,16,32,2304]{3,2,0,1:T(8,128)(2,1)}, u32[]{:S(2)}, u32[]{:S(2)}) %all-to-all-start.2) | async-done | bytes 2359328 | tf_op jit(solution)/shard_map/all_to_all | solution.py:83
  277.0 12.3 %all-to-all-start.1 = ((bf16[1,16,32,768]{3,2,0,1:T(8,128)(2,1)}), bf16[1,16,32,768]{3,2,0,1:T(8,128)(2,1)S(1)}, u32[]{:S(2)}, u32[]{:S(2)}) async-start(bf16[1,16,32,768]{3,2,0,1:T(8,128)(2,1)} %bitcast.17), calls=%async_computation.1 | async-start | bytes 1572864 | tf_op jit(solution)/shard_map/all_to_all | solution.py:84
  289.3 0.8 fusion.26
  290.1 0.8 reshape.120
  290.9 6.0 %reshape_reshape.3 = bf16[2,8,32,3,6,128]{5,4,3,2,1,0:T(8,128)(2,1)} reshape(bf16[1,16,32,2304]{3,2,0,1:T(8,128)(2,1)} %all-to-all-done.2) | data formatting | bytes 4718592 | tf_op jit(solution)/shard_map/reshape;reshape | solution.py:36
  296.9 2.4 fusion.32
  299.3 1.3 fusion.36
  301.3 1.1 fusion.16
  302.8 5.2 %all-to-all-done.1 = bf16[1,16,32,768]{3,2,0,1:T(8,128)(2,1)S(1)} async-done(((bf16[1,16,32,768]{3,2,0,1:T(8,128)(2,1)}), bf16[1,16,32,768]{3,2,0,1:T(8,128)(2,1)S(1)}, u32[]{:S(2)}, u32[]{:S(2)}) %all-to-all-start.1) | async-done | bytes 786464 | tf_op jit(solution)/shard_map/all_to_all | solution.py:84
  308.0 7.7 %fusion.12 = f32[512,3072]{1,0:T(8,128)S(1)} fusion(bf16[1536,3072]{0,1:T(8,128)(2,1)} %all-gather.5.cloned.1.call-done, bf16[512,768]{1,0:T(8,128)(2,1)S(1)} %bitcast.104, bf16[512,768]{1,0:T(8,128)(2,1)S(1)} %bitcast.105), kind=kOutput, calls=%fused_computation.19 | convolution fusion | flops 4834983936 | bytes 17301504 | tf_op jit(solution)/shard_map/dot_general | solution.py:95
  315.7 1.0 fusion.37
  317.7 1.6 add_convert_fusion
  319.4 1.1 convolution_convert_fusion.1
  320.9 12.1 %all_to_all.16 = bf16[16,2,1024]{2,1,0:T(2,128)(2,1)S(1)} all-to-all(bf16[16,2,1024]{2,1,0:T(2,128)(2,1)S(1)} %reshape.121), channel_id=1, replica_groups=mesh['groups'=2,'seq'=16] {'seq'}, dimensions={0} | all-to-all | bytes 131072 | tf_op jit(solution)/shard_map/all_to_all | solution.py:119
  333.1 0.9 reshape.115
  (54 shorter events, 5.3 us)
Async XLA Ops:
  6.5 14.2 %copy-start = (bf16[2,128,3072]{2,1,0:T(8,128)(2,1)S(1)}, bf16[2,128,3072]{2,1,0:T(8,128)(2,1)}, u32[]{:S(2)}) copy-start(bf16[2,128,3072]{2,1,0:T(8,128)(2,1)} %param.9) | copy-start | bytes 4718596
  6.5 149.5 %all-gather.3.cloned.1.call-start = ((), (), s32[]{:S(2)}) async-start(), calls=%async_computation.4 | async-start | bytes 30081024 | tf_op jit(solution)/shard_map/all_gather | solution.py:70
  7.3 295.6 %all-gather.5.cloned.1.call-start = ((), (), s32[]{:S(2)}) async-start(), calls=%async_computation.5 | async-start | bytes 10027008 | tf_op jit(solution)/shard_map/all_gather | solution.py:97
  10.2 193.6 %all-to-all-start = ((bf16[16,2,1024]{2,1,0:T(2,128)(2,1)}), bf16[16,2,1024]{2,1,0:T(2,128)(2,1)S(1)}, u32[]{:S(2)}, u32[]{:S(2)}) async-start(bf16[16,2,1024]{2,1,0:T(2,128)(2,1)} %reshape.119), calls=%async_computation | async-start | bytes 131072 | tf_op jit(solution)/shard_map/all_to_all | solution.py:85
  17.7 3.0 copy-start.9
  197.8 10.9 %copy-start.10 = (s32[2,128]{1,0:T(2,128)S(1)}, s32[2,128]{1,0:T(2,128)}, u32[]{:S(2)}) copy-start(s32[2,128]{1,0:T(2,128)} %param.10) | copy-start | bytes 3076
  203.8 5.1 %copy-start.7 = (bf16[16,2,1024]{2,1,0:T(2,128)(2,1)}, bf16[16,2,1024]{2,1,0:T(2,128)(2,1)S(1)}, u32[]{:S(2)}) copy-start(bf16[16,2,1024]{2,1,0:T(2,128)(2,1)S(1)} %all-to-all-done) | copy-start | bytes 196612
  203.8 73.2 %all-to-all-start.2 = ((bf16[1,16,32,2304]{3,2,0,1:T(8,128)(2,1)}), bf16[1,16,32,2304]{3,2,0,1:T(8,128)(2,1)}, u32[]{:S(2)}, u32[]{:S(2)}) async-start(bf16[1,16,32,2304]{3,2,0,1:T(8,128)(2,1)} %bitcast.101), calls=%async_computation.2 | async-start | bytes 4718592 | tf_op jit(solution)/shard_map/all_to_all | solution.py:83
  217.6 72.5 %copy-start.8 = (bf16[16,2,1024]{2,1,0:T(2,128)(2,1)S(1)}, bf16[16,2,1024]{2,1,0:T(2,128)(2,1)}, u32[]{:S(2)}) copy-start(bf16[16,2,1024]{2,1,0:T(2,128)(2,1)} %copy-done.7) | copy-start | bytes 196612
  277.0 31.0 %all-to-all-start.1 = ((bf16[1,16,32,768]{3,2,0,1:T(8,128)(2,1)}), bf16[1,16,32,768]{3,2,0,1:T(8,128)(2,1)S(1)}, u32[]{:S(2)}, u32[]{:S(2)}) async-start(bf16[1,16,32,768]{3,2,0,1:T(8,128)(2,1)} %bitcast.17), calls=%async_computation.1 | async-start | bytes 1572864 | tf_op jit(solution)/shard_map/all_to_all | solution.py:84
  308.0 7.7 %copy-start.2 = (bf16[64,3072]{1,0:T(8,128)(2,1)S(1)}, bf16[64,3072]{1,0:T(8,128)(2,1)}, u32[]{:S(2)}) copy-start(bf16[64,3072]{1,0:T(8,128)(2,1)} %param.12) | copy-start | bytes 1179652
  308.0 7.7 %copy-start.4 = (f32[16,3072]{1,0:T(8,128)S(1)}, f32[16,3072]{1,0:T(8,128)}, u32[]{:S(2)}) copy-start(f32[16,3072]{1,0:T(8,128)} %get-tuple-element.10) | copy-start | bytes 589828
  308.0 7.7 %copy-start.5 = (bf16[16,1,32,64]{3,2,1,0:T(8,128)(2,1)S(1)}, bf16[16,1,32,64]{3,2,1,0:T(8,128)(2,1)}, u32[]{:S(2)}) copy-start(bf16[16,1,32,64]{3,2,1,0:T(8,128)(2,1)} %reshape.120) | copy-start | bytes 196612
  316.8 0.9 copy-start.3
  317.6 1.8 copy-start.6
  317.6 16.4 %copy-start.1 = (bf16[2,128,3072]{2,1,0:T(8,128)(2,1)S(1)}, bf16[2,128,3072]{2,1,0:T(8,128)(2,1)}, u32[]{:S(2)}) copy-start(bf16[2,128,3072]{2,1,0:T(8,128)(2,1)} %param.9) | copy-start | bytes 4718596
Sparse Core Ops, SparseCore 0:
  8.9 147.1 all-gather.2
  158.4 115.3 all-gather.4
where the time goes:
time: 342 us; the launch traced here: 341 us
  waiting for transfers between devices  195 us (57%)
  matrix products  45.7 us (13%)
  local copies, waits for them, and re-layouts  37.8 us (11%)
  starting transfers between devices  24.6 us (7%)
  between operations  13.8 us (4%)
  blocking collectives  12.1 us (4%)
  other arithmetic  11.4 us (3%)
    all_gather x1, waiting for transfers between devices, per_device(): lax.all_gather(w_qkv, 'seq', axis=1, tiled=True)  132 us
    all_to_all x1, waiting for transfers between devices, per_device(): lax.all_to_all(temporal_rows, 'seq', split_axis=1, concat_axis=0, tiled=T...  56.8 us
    dot_general x1, matrix products, per_device(): jnp.dot(rows, lax.all_gather(w_qkv, 'seq', axis=1, tiled=True), preferred...  24.7 us
    all_to_all x1, starting transfers between devices, per_device(): lax.all_to_all(spatial_rows, 'seq', split_axis=1, concat_axis=0, tiled=True)  12.3 us
    all_to_all x1, blocking collectives, per_device(): lax.all_to_all(both_halves.astype(jnp.bfloat16), 'seq', split_axis=0, con...  12.1 us
    convert_element_type x1, local copies, waits for them, and re-layouts, per_device(): projected = jnp.dot(rows, lax.all_gather(w_qkv, 'seq', axis=1, tiled=True...  8.94 us
    slice x2, local copies, waits for them, and re-layouts, per_device(): projected[:positions, :, SHEADS:].reshape(1, count, span, 3 * THEADS * HDIM)  8.03 us
    dot_general x1, matrix products, per_device(): jnp.dot(joined, lax.all_gather(w_attn_out, 'seq', axis=1, tiled=True), pr...  7.7 us
  transfers between devices with their start and end apart: 5, of which 3 were waited for; matrix products, arithmetic and copies ran while one was open for 24% of the time, Pallas kernels for 0%

commit v1 on v0

--- a/solution.py
+++ b/solution.py
@@ -81,7 +81,12 @@
     temporal_pos, spatial_pos, latent_pos = temporal_local(
         (
             lax.all_to_all(temporal_rows, "seq", split_axis=1, concat_axis=0, tiled=True),
-            lax.all_to_all(spatial_rows, "seq", split_axis=1, concat_axis=0, tiled=True),
+            jnp.concatenate(
+                lax.all_to_all(
+                    jnp.stack(jnp.split(spatial_rows, lax.axis_size("seq"), axis=1)), "seq", 0, 0
+                ),
+                axis=0,
+            ),
             lax.all_to_all(latent_rows, "seq", split_axis=1, concat_axis=0, tiled=True),
         )
     )

time: 342 us -> 342 us (level)
  waiting for transfers between devices: 195 us -> 179 us
  local copies, waits for them, and re-layouts: 37.8 us -> 46 us
  matrix products: 45.7 us -> 51.6 us
    all_to_all x1, waiting for transfers between devices: 56.8 us -> 40.2 us  [per_device(): lax.all_to_all(temporal_rows, 'seq', split_axis=1, concat_axis=0, tiled=T...]
    unnamed x27 -> x38, local copies, waits for them, and re-layouts: 2.15 us -> 10.8 us
    dot_general x1, matrix products: 3.02 us -> 6.69 us  [attend(): jnp.einsum('qhe,khe->hqk', query, keys, preferred_element_type=jnp.float32)]
  transfers between devices with their start and end apart: 5 -> 5, of which waited for: 3 -> 3; matrix products, arithmetic and copies ran while one was open for 24% -> 29% of each run, Pallas kernels for 0% -> 0%
where the time goes in v1:
time: 342 us; the launch traced here: 341 us
  waiting for transfers between devices  179 us (52%)
  matrix products  51.6 us (15%)
  local copies, waits for them, and re-layouts  46 us (13%)
  starting transfers between devices  24.5 us (7%)
  other arithmetic  14.5 us (4%)
  between operations  13.8 us (4%)
  blocking collectives  12.1 us (4%)
    all_gather x1, waiting for transfers between devices, per_device(): lax.all_gather(w_qkv, 'seq', axis=1, tiled=True)  131 us
    all_to_all x1, waiting for transfers between devices, per_device(): lax.all_to_all(temporal_rows, 'seq', split_axis=1, concat_axis=0, tiled=T...  40.2 us
    dot_general x1, matrix products, per_device(): jnp.dot(rows, lax.all_gather(w_qkv, 'seq', axis=1, tiled=True), preferred...  24.8 us
    all_to_all x1, starting transfers between devices, per_device(): lax.all_to_all(jnp.stack(jnp.split(spatial_rows, lax.axis_size('seq'), ax...  12.4 us
    all_to_all x1, blocking collectives, per_device(): lax.all_to_all(both_halves.astype(jnp.bfloat16), 'seq', split_axis=0, con...  12.1 us
    unnamed x38, local copies, waits for them, and re-layouts  10.8 us
    convert_element_type x1, local copies, waits for them, and re-layouts, per_device(): projected = jnp.dot(rows, lax.all_gather(w_qkv, 'seq', axis=1, tiled=True...  8.91 us
    slice x2, local copies, waits for them, and re-layouts, per_device(): projected[:positions, :, SHEADS:].reshape(1, count, span, 3 * THEADS * HDIM)  8 us
  transfers between devices with their start and end apart: 5, of which 3 were waited for; matrix products, arithmetic and copies ran while one was open for 29% of the time, Pallas kernels for 0%

profile of v1, /device:TPU:0, one launch (start us, length us, event | category | flops | bytes accessed | tf_op | source)
XLA Modules:
  0.0 341.1 jit_solution(6613459880786389361)
XLA Ops:
  8.0 1.3 reduce
  9.4 0.8 reshape.111
  10.2 7.4 %all-to-all-start = ((bf16[16,2,1024]{2,1,0:T(2,128)(2,1)}), bf16[16,2,1024]{2,1,0:T(2,128)(2,1)S(1)}, u32[]{:S(2)}, u32[]{:S(2)}) async-start(bf16[16,2,1024]{2,1,0:T(2,128)(2,1)} %reshape.111), calls=%async_computation | async-start | bytes 131072 | tf_op jit(solution)/shard_map/all_to_all | solution.py:90
  18.4 2.1 fusion.51
  20.6 0.8 multiply_reduce_fusion.1
  21.8 3.3 add_convert_fusion.1
  25.0 131.1 %all-gather.3.cloned.1.call-done = bf16[3072,4608]{0,1:T(8,128)(2,1)} async-done(((bf16[3072,288]{0,1:T(8,128)(2,1)}), bf16[3072,4608]{0,1:T(8,128)(2,1)}) %all-gather.3.cloned.1.call-update) | async-done | bytes 28311568 | tf_op jit(solution)/shard_map/all_gather | solution.py:70
  156.1 24.8 %convolution_convert_fusion = bf16[640,4608]{1,0:T(8,128)(2,1)} fusion(bf16[3072,4608]{0,1:T(8,128)(2,1)} %all-gather.3.cloned.1.call-done, bf16[128,3072]{1,0:T(8,128)(2,1)S(1)} %dynamic-slice_bitcast_fusion, bf16[512,3072]{1,0:T(8,128)(2,1)} %add_convert_fusion.1), kind=kOutput, calls=%fused_computation | convolution fusion | flops 18130206720 | bytes 38141952 | tf_op jit(solution)/shard_map/dot_general | solution.py:69
  180.9 8.9 %copy.45 = bf16[640,4608]{0,1:T(8,128)(2,1)} copy(bf16[640,4608]{1,0:T(8,128)(2,1)} %convolution_convert_fusion) | data formatting | bytes 11796480 | tf_op jit(solution)/shard_map/convert_element_type | solution.py:71
  189.8 6.7 %fusion = (f32[6,512]{1,0:T(8,128)S(1)}, f32[6,512,640]{2,1,0:T(8,128)}) fusion(pred[640]{0:T(1024)(128)(4,1)S(1)} %concatenate.14, bf16[640,3,12,128]{0,3,2,1:T(8,128)(2,1)} %bitcast.160), kind=kOutput, calls=%fused_computation.3 | convolution fusion | flops 509211648 | bytes 9646720 | tf_op jit(solution)/shard_map/qhe,khe->hqk/dot_general | solution.py:22
  196.5 3.3 slice.78
  199.8 4.7 %copy.49 = bf16[512,3,6,128]{3,2,1,0:T(8,128)(2,1)} copy(bf16[512,3,6,128]{0,3,2,1:T(8,128)(2,1)} %slice.78) | data formatting | bytes 4718592 | tf_op jit(solution)/shard_map/slice | solution.py:78
  204.5 5.9 %reshape.104 = bf16[1,16,32,2304]{3,2,1,0:T(8,128)(2,1)} reshape(bf16[512,3,6,128]{3,2,1,0:T(8,128)(2,1)} %copy.49) | data formatting | bytes 4718592 | tf_op jit(solution)/shard_map/reshape | solution.py:78
  210.4 4.7 %all-to-all-start.2 = ((bf16[1,16,32,2304]{3,2,0,1:T(8,128)(2,1)}), bf16[1,16,32,2304]{3,2,0,1:T(8,128)(2,1)}, u32[]{:S(2)}, u32[]{:S(2)}) async-start(bf16[1,16,32,2304]{3,2,0,1:T(8,128)(2,1)} %bitcast.164), calls=%async_computation.2 | async-start | bytes 4718592 | tf_op jit(solution)/shard_map/all_to_all | solution.py:83
  215.1 4.4 %fusion.1 = f32[6,512]{1,0:T(8,128)S(1)} fusion(f32[6,512,640]{2,1,0:T(8,128)} %get-tuple-element.22, f32[6,512]{1,0:T(8,128)S(1)} %get-tuple-element.21, pred[640]{0:T(1024)(128)(4,1)S(1)} %concatenate.14), kind=kLoop, calls=%fused_computation.9 | loop fusion | flops 7861248 | bytes 7889536 | tf_op jit(solution)/shard_map/reduce_sum | solution.py:28
  219.5 5.6 %fusion.17 = bf16[512,6,128]{0,2,1:T(8,128)(2,1)S(1)} fusion(f32[6,512,640]{2,1,0:T(8,128)} %get-tuple-element.22, f32[6,512]{1,0:T(8,128)S(1)} %get-tuple-element.21, pred[640]{0:T(1024)(128)(4,1)S(1)} %concatenate.14, bf16[640,3,12,128]{0,3,2,1:T(8,128)(2,1)} %bitcast.162, f32[512,6]{0,1:T(8,128)S(1)} %bitcast.174), kind=kOutput, calls=%fused_computation.26 | convolution fusion | flops 511967232 | bytes 9659008 | tf_op jit(solution)/shard_map/hqk,khe->qhe/dot_general | solution.py:30
  225.9 0.9 reshape.103
  236.8 40.2 %all-to-all-done.2 = bf16[1,16,32,2304]{3,2,0,1:T(8,128)(2,1)} async-done(((bf16[1,16,32,2304]{3,2,0,1:T(8,128)(2,1)}), bf16[1,16,32,2304]{3,2,0,1:T(8,128)(2,1)}, u32[]{:S(2)}, u32[]{:S(2)}) %all-to-all-start.2) | async-done | bytes 2359328 | tf_op jit(solution)/shard_map/all_to_all | solution.py:83
  277.0 12.4 %all-to-all-start.1 = ((bf16[16,1,1,32,768]{4,3,2,1,0:T(8,128)(2,1)}), bf16[16,1,1,32,768]{4,3,2,1,0:T(8,128)(2,1)}, u32[]{:S(2)}, u32[]{:S(2)}) async-start(bf16[16,1,1,32,768]{4,3,2,1,0:T(8,128)(2,1)} %fusion.28), calls=%async_computation.1 | async-start | bytes 1572864 | tf_op jit(solution)/shard_map/all_to_all | solution.py:85
  289.4 0.8 fusion.26
  290.3 6.0 %reshape_reshape.7 = bf16[2,8,32,3,6,128]{5,4,3,2,1,0:T(8,128)(2,1)} reshape(bf16[1,16,32,2304]{3,2,0,1:T(8,128)(2,1)} %all-to-all-done.2) | data formatting | bytes 4718592 | tf_op jit(solution)/shard_map/reshape;reshape | solution.py:36
  296.4 2.4 fusion.48
  298.8 1.3 fusion.52
  300.7 1.1 fusion.16
  302.2 5.9 %all-to-all-done.1 = bf16[16,1,1,32,768]{4,3,2,1,0:T(8,128)(2,1)} async-done(((bf16[16,1,1,32,768]{4,3,2,1,0:T(8,128)(2,1)}), bf16[16,1,1,32,768]{4,3,2,1,0:T(8,128)(2,1)}, u32[]{:S(2)}, u32[]{:S(2)}) %all-to-all-start.1) | async-done | bytes 786464 | tf_op jit(solution)/shard_map/all_to_all | solution.py:85
  308.1 7.9 %fusion.12 = f32[512,3072]{1,0:T(8,128)S(1)} fusion(bf16[1536,3072]{0,1:T(8,128)(2,1)} %all-gather.5.cloned.1.call-done, bf16[512,768]{1,0:T(8,128)(2,1)S(1)} %bitcast.167, bf16[512,768]{1,0:T(8,128)(2,1)} %bitcast.33), kind=kOutput, calls=%fused_computation.19 | convolution fusion | flops 4834983936 | bytes 17301504 | tf_op jit(solution)/shard_map/dot_general | solution.py:100
  316.1 1.0 fusion.53
  317.1 0.8 multiply_reduce_fusion
  318.0 1.6 add_convert_fusion
  319.7 1.1 convolution_convert_fusion.1
  321.2 12.1 %all_to_all.32 = bf16[16,2,1024]{2,1,0:T(2,128)(2,1)S(1)} all-to-all(bf16[16,2,1024]{2,1,0:T(2,128)(2,1)S(1)} %reshape.113), channel_id=1, replica_groups=mesh['groups'=2,'seq'=16] {'seq'}, dimensions={0} | all-to-all | bytes 131072 | tf_op jit(solution)/shard_map/all_to_all | solution.py:124
  333.4 0.9 reshape.107
  (66 shorter events, 15.3 us)
Async XLA Ops:
  6.5 14.8 %copy-start = (bf16[2,128,3072]{2,1,0:T(8,128)(2,1)S(1)}, bf16[2,128,3072]{2,1,0:T(8,128)(2,1)}, u32[]{:S(2)}) copy-start(bf16[2,128,3072]{2,1,0:T(8,128)(2,1)} %param.9) | copy-start | bytes 4718596
  6.5 149.5 %all-gather.3.cloned.1.call-start = ((), (), s32[]{:S(2)}) async-start(), calls=%async_computation.4 | async-start | bytes 30081024 | tf_op jit(solution)/shard_map/all_gather | solution.py:70
  7.3 295.0 %all-gather.5.cloned.1.call-start = ((), (), s32[]{:S(2)}) async-start(), calls=%async_computation.5 | async-start | bytes 10027008 | tf_op jit(solution)/shard_map/all_gather | solution.py:102
  10.2 200.3 %all-to-all-start = ((bf16[16,2,1024]{2,1,0:T(2,128)(2,1)}), bf16[16,2,1024]{2,1,0:T(2,128)(2,1)S(1)}, u32[]{:S(2)}, u32[]{:S(2)}) async-start(bf16[16,2,1024]{2,1,0:T(2,128)(2,1)} %reshape.111), calls=%async_computation | async-start | bytes 131072 | tf_op jit(solution)/shard_map/all_to_all | solution.py:90
  18.4 2.9 copy-start.8
  210.4 9.1 %copy-start.6 = (bf16[16,2,1024]{2,1,0:T(2,128)(2,1)}, bf16[16,2,1024]{2,1,0:T(2,128)(2,1)S(1)}, u32[]{:S(2)}) copy-start(bf16[16,2,1024]{2,1,0:T(2,128)(2,1)S(1)} %all-to-all-done) | copy-start | bytes 196612
  210.4 66.6 %all-to-all-start.2 = ((bf16[1,16,32,2304]{3,2,0,1:T(8,128)(2,1)}), bf16[1,16,32,2304]{3,2,0,1:T(8,128)(2,1)}, u32[]{:S(2)}, u32[]{:S(2)}) async-start(bf16[1,16,32,2304]{3,2,0,1:T(8,128)(2,1)} %bitcast.164), calls=%async_computation.2 | async-start | bytes 4718592 | tf_op jit(solution)/shard_map/all_to_all | solution.py:83
  225.2 65.0 %copy-start.7 = (bf16[16,2,1024]{2,1,0:T(2,128)(2,1)S(1)}, bf16[16,2,1024]{2,1,0:T(2,128)(2,1)}, u32[]{:S(2)}) copy-start(bf16[16,2,1024]{2,1,0:T(2,128)(2,1)} %copy-done.6) | copy-start | bytes 196612
  277.0 31.1 %all-to-all-start.1 = ((bf16[16,1,1,32,768]{4,3,2,1,0:T(8,128)(2,1)}), bf16[16,1,1,32,768]{4,3,2,1,0:T(8,128)(2,1)}, u32[]{:S(2)}, u32[]{:S(2)}) async-start(bf16[16,1,1,32,768]{4,3,2,1,0:T(8,128)(2,1)} %fusion.28), calls=%async_computation.1 | async-start | bytes 1572864 | tf_op jit(solution)/shard_map/all_to_all | solution.py:85
  308.1 7.9 %copy-start.2 = (bf16[64,3072]{1,0:T(8,128)(2,1)S(1)}, bf16[64,3072]{1,0:T(8,128)(2,1)}, u32[]{:S(2)}) copy-start(bf16[64,3072]{1,0:T(8,128)(2,1)} %param.12) | copy-start | bytes 1179652
  308.1 7.9 %copy-start.4 = (f32[16,3072]{1,0:T(8,128)S(1)}, f32[16,3072]{1,0:T(8,128)}, u32[]{:S(2)}) copy-start(f32[16,3072]{1,0:T(8,128)} %get-tuple-element.10) | copy-start | bytes 589828
  317.1 0.9 copy-start.3
  317.9 1.8 copy-start.5
  317.9 16.4 %copy-start.1 = (bf16[2,128,3072]{2,1,0:T(8,128)(2,1)S(1)}, bf16[2,128,3072]{2,1,0:T(8,128)(2,1)}, u32[]{:S(2)}) copy-start(bf16[2,128,3072]{2,1,0:T(8,128)(2,1)} %param.9) | copy-start | bytes 4718596
Sparse Core Ops, SparseCore 0:
  8.9 147.1 all-gather.2
  158.4 111.9 all-gather.4
